TPU v7x, 256 devices: a whole 4x4x8 slice. The times are simulated.
256 devices in a mesh: branch: 64 (over x, z, core), sub: 4 (over y).
Axes of the slice: x: 4, y: 4, z: 8, core: 2. Of those that a mesh axis runs over, the one named last changes fastest.
Arguments:
- vectors: float32 [9216, 16, 128], P(('branch', 'sub')), may hold values from -6 to 6
- leaf_basis: float32 [9216, 64, 128], P(('branch', 'sub')), may hold values from -0.5 to 0.5
- near_index: int32 [9216, 3], P(('branch', 'sub')), may hold values from 0 to 9215, as said below
- near_blocks: float32 [9216, 3, 128, 128], P(('branch', 'sub')), may hold values from -0.3125 to 0.3125
- coupling_index: int32 [9216, 4], P(('branch', 'sub')), may hold values from 0 to 9215, as said below
- coupling_blocks: float32 [9216, 4, 64, 64], P(('branch', 'sub')), may hold values from -0.375 to 0.375
- leaf_transfer: float32 [9216, 64, 64], P(('branch', 'sub')), may hold values from -0.125 to 0.125
- cluster_transfer: float32 [256, 64, 64], P(('branch', 'sub')), may hold values from -0.375 to 0.375
- branch_index: int32 [64, 16], P('branch'), may hold values from 0 to 63, as said below
- branch_blocks: float32 [64, 16, 64, 64], P('branch'), may hold values from -0.1875 to 0.1875
Outputs:
- product: float32 [9216, 16, 128], P(('branch', 'sub'))
Inputs may be any that keep to these rules, and one draw needn't show every extreme that they name: `near_index`: entry 0 of row l is l itself; every entry of row l lies within 36 of l. `coupling_index`: every entry of row l lies within 36 of l. `branch_index`: the entries of a row are distinct and differ from the row's own branch cluster.
All inputs are finite; a program needn't handle non-finite values.
Results may differ from a plain program's by a relative error of at most 0.000067.
Values sent between devices are 32-bit elements; how exact they have to be, the bound alone decides.
A program may use at most 64 MiB of HBM per device.

v0:
```python
import jax
import jax.numpy as jnp
from jax import lax
from jax.sharding import PartitionSpec as P

highest = lax.Precision.HIGHEST


def with_halo(block, sides, width):
    for axis, dim in sides:
        count = lax.axis_size(axis)
        forward = [(i, i + 1) for i in range(count - 1)]
        backward = [(target, source) for source, target in forward]
        low = lax.ppermute(
            lax.slice_in_dim(block, block.shape[dim] - width, None, axis=dim), axis, forward
        )
        high = lax.ppermute(lax.slice_in_dim(block, 0, width, axis=dim), axis, backward)
        block = jnp.concatenate([low, block, high], axis=dim)
    return block


def per_device(
    vectors,
    leaf_basis,
    near_index,
    near_blocks,
    coupling_index,
    coupling_blocks,
    leaf_transfer,
    cluster_transfer,
    branch_index,
    branch_blocks,
):
    leaf_count = vectors.shape[0]
    coeffs = jnp.einsum("lrp,lvp->lvr", leaf_basis, vectors, precision=highest)
    wide_points = with_halo(vectors, ((("branch", "sub"), 0),), leaf_count)
    wide_coeffs = with_halo(coeffs, ((("branch", "sub"), 0),), leaf_count)
    anchor = lax.axis_index(("branch", "sub")) * leaf_count - leaf_count
    near_rows = jnp.take(wide_points, near_index - anchor, axis=0)
    near_part = jnp.einsum("lkpq,lkvq->lvp", near_blocks, near_rows, precision=highest)
    coupled_rows = jnp.take(wide_coeffs, coupling_index - anchor, axis=0)
    leaf_far = jnp.einsum("lkrs,lkvs->lvr", coupling_blocks, coupled_rows, precision=highest)
    cluster = jnp.einsum("crs,cvs->vr", leaf_transfer, coeffs, precision=highest)
    share = jnp.einsum("rt,vt->vr", cluster_transfer[0], cluster, precision=highest)
    branch_node = lax.psum(share, "sub")
    nodes = lax.all_gather(branch_node[None], "branch", axis=0, tiled=True)
    chosen = jnp.take(nodes, branch_index[0], axis=0)
    branch_far = jnp.einsum("krs,kvs->vr", branch_blocks[0], chosen, precision=highest)
    cluster_down = jnp.einsum("rt,vr->vt", cluster_transfer[0], branch_far, precision=highest)
    leaf_total = leaf_far + jnp.einsum(
        "crs,vr->cvs", leaf_transfer, cluster_down, precision=highest
    )
    return near_part + jnp.einsum("lrp,lvr->lvp", leaf_basis, leaf_total, precision=highest)


def solution(mesh):
    in_specs = (
        P(("branch", "sub"), None, None),
        P(("branch", "sub"), None, None),
        P(("branch", "sub"), None),
        P(("branch", "sub"), None, None, None),
        P(("branch", "sub"), None),
        P(("branch", "sub"), None, None, None),
        P(("branch", "sub"), None, None),
        P(("branch", "sub"), None, None),
        P("branch", None),
        P("branch", None, None, None),
    )
    out_specs = P(("branch", "sub"), None, None)
    return jax.shard_map(
        per_device, mesh=mesh, in_specs=in_specs, out_specs=out_specs, check_vma=False
    )
```

profile of v0, /device:TPU:1, one launch (start us, length us, event | category | flops | bytes accessed | tf_op | source)
XLA Modules:
  0.0 115.5 jit_solution(5684814676402167963)
XLA Ops:
  0.0 1.2 %copy-done = f32[36,64,128]{2,1,0:T(8,128)S(1)} copy-done((f32[36,64,128]{2,1,0:T(8,128)S(1)}, f32[36,64,128]{2,1,0:T(8,128)}, u32[]{:S(2)}) %copy-start) | copy-done | bytes 1179672
  1.3 2.9 %fusion.21 = f32[36,16,64]{2,1,0:T(8,128)S(1)} fusion(f32[36,16,128]{2,1,0:T(8,128)} %param.10, f32[36,64,128]{2,1,0:T(8,128)S(1)} %copy-done), kind=kOutput, calls=%fused_computation.41 | convolution fusion | flops 56623104 | bytes 1622016 | tf_op jit(solution)/shard_map/lrp,lvp->lvr/dot_general | solution.py:35
  4.2 6.2 %collective-permute-start.3 = (f32[36,16,64]{2,1,0:T(8,128)S(1)}, f32[36,16,64]{2,1,0:T(8,128)}, u32[]{:S(2)}, u32[]{:S(2)}) collective-permute-start(f32[36,16,64]{2,1,0:T(8,128)S(1)} %fusion.21), channel_id=1, source_target_pairs={{1,0},{2,1},{3,2},{4,3},{5,4},{6,5},{7,6},{8,7},{9,8},{10,9},{11,1... | collective-permute-start | bytes 442376 | tf_op jit(solution)/shard_map/ppermute | solution.py:17
  10.3 1.9 %collective-permute-start.2 = (f32[36,16,64]{2,1,0:T(8,128)S(1)}, f32[36,16,64]{2,1,0:T(8,128)}, u32[]{:S(2)}, u32[]{:S(2)}) collective-permute-start(f32[36,16,64]{2,1,0:T(8,128)S(1)} %fusion.21), channel_id=1, source_target_pairs={{0,1},{1,2},{2,3},{3,4},{4,5},{5,6},{6,7},{7,8},{8,9},{9,10},{10,1... | collective-permute-start | bytes 442376 | tf_op jit(solution)/shard_map/ppermute | solution.py:14
  12.3 4.9 %collective-permute-start.1 = (f32[36,16,128]{2,1,0:T(8,128)}, f32[36,16,128]{2,1,0:T(8,128)}, u32[]{:S(2)}, u32[]{:S(2)}) collective-permute-start(f32[36,16,128]{2,1,0:T(8,128)} %param.10), channel_id=1, source_target_pairs={{1,0},{2,1},{3,2},{4,3},{5,4},{6,5},{7,6},{8,7},{9,8},{10,9},{11,1... | collective-permute-start | bytes 884744 | tf_op jit(solution)/shard_map/ppermute | solution.py:17
  17.1 1.9 %collective-permute-start = (f32[36,16,128]{2,1,0:T(8,128)}, f32[36,16,128]{2,1,0:T(8,128)}, u32[]{:S(2)}, u32[]{:S(2)}) collective-permute-start(f32[36,16,128]{2,1,0:T(8,128)} %param.10), channel_id=1, source_target_pairs={{0,1},{1,2},{2,3},{3,4},{4,5},{5,6},{6,7},{7,8},{8,9},{9,10},{10,1... | collective-permute-start | bytes 884744 | tf_op jit(solution)/shard_map/ppermute | solution.py:14
  19.5 0.1 reshape.46
  19.6 1.0 convolution_bitcast_fusion.2
  20.6 0.2 convolution_bitcast_fusion.5
  20.8 10.3 %psum.7 = f32[1,16,64]{2,1,0:T(8,128)S(1)} all-reduce(f32[1,16,64]{2,1,0:T(8,128)S(1)} %convolution_bitcast_fusion.5), channel_id=1, replica_groups=mesh['branch'=64,'sub'=4] {'sub'}, use_global_device_ids=true, to_apply=%region_0.1 | all-reduce | flops 1024 | bytes 8192 | tf_op jit(solution)/shard_map/psum | solution.py:45
  31.1 56.7 %all_gather.3 = f32[64,16,64]{2,1,0:T(8,128)S(1)} all-gather(f32[1,16,64]{2,1,0:T(8,128)S(1)} %psum.7), channel_id=1, replica_groups=mesh['branch'=64,'sub'=4] {'branch'}, dimensions={0}, use_global_device_ids=true | all-gather | bytes 266240 | tf_op jit(solution)/shard_map/all_gather | solution.py:46
  87.8 0.6 gather_fusion.2
  88.3 1.6 %convolution_bitcast_fusion.4 = f32[16,64]{1,0:T(8,128)S(1)} fusion(f32[1,16,64,64]{3,2,1,0:T(8,128)} %param.19, f32[16,16,64]{2,1,0:T(8,128)S(1)} %gather_fusion.2, pred[16]{0:T(512)(128)(4,1)S(1)} %compare_and_fusion), kind=kOutput, calls=%fused_computation.12 | convolution fusion | flops 12599296 | bytes 331792 | tf_op jit(solution)/shard_map/krs,kvs->vr/dot_general | solution.py:48
  90.0 0.7 copy.20
  90.7 0.7 copy.18
  91.4 0.1 convolution_bitcast_fusion.3
  91.5 1.1 pad_maximum_fusion.1
  92.7 1.8 %gather_fusion.1 = f32[144,16,64]{2,1,0:T(8,128)} fusion(f32[108,16,64]{2,1,0:T(8,128)S(1)} %pad_maximum_fusion.1, s32[1024]{0:T(1024)S(1)} %pad_clamp_fusion.1), kind=kCustom, calls=%fused_computation.1 | custom fusion | bytes 1180224 | tf_op jit(solution)/shard_map/jit(_take)/gather | solution.py:41
  94.5 6.7 %fusion.3 = f32[36,16,64]{2,1,0:T(8,128)S(1)} fusion(f32[36,4,64,64]{3,2,1,0:T(8,128)} %param.15, f32[36,4,16,64]{3,2,1,0:T(8,128)} %bitcast.46, pred[36,4]{1,0:T(8,128)(4,1)S(1)} %copy-done.4), kind=kOutput, calls=%fused_computation.8 | convolution fusion | flops 113393664 | bytes 3096720 | tf_op jit(solution)/shard_map/lkrs,lkvs->lvr/dot_general | solution.py:42
  101.2 0.7 fusion.2
  101.9 1.2 %pad_maximum_fusion = f32[108,16,128]{2,1,0:T(8,128)S(1)} fusion(f32[36,16,128]{2,1,0:T(8,128)} %collective-permute-done.1, f32[36,16,128]{2,1,0:T(8,128)} %param.10, f32[36,16,128]{2,1,0:T(8,128)} %collective-permute-done), kind=kLoop, calls=%fused_computation.14 | loop fusion | flops 442368 | bytes 1769472 | tf_op jit(solution)/shard_map/concatenate | solution.py:18
  103.1 0.7 gather_fusion
  103.8 9.8 %convolution_bitcast_fusion.1 = f32[36,16,128]{2,1,0:T(8,128)S(1)} fusion(f32[36,3,128,128]{3,2,1,0:T(8,128)} %param.13, f32[36,3,16,128]{3,2,1,0:T(8,128)S(1)} %bitcast.47, pred[36,3]{1,0:T(8,128)(4,1)S(1)} %copy-done.3), kind=kOutput, calls=%fused_computation.9 | convolution fusion | flops 339959808 | bytes 8257644 | tf_op jit(solution)/shard_map/lkpq,lkvq->lvp/dot_general | solution.py:40
  113.6 1.9 %convolution_add_fusion = f32[36,16,128]{2,1,0:T(8,128)} fusion(f32[36,16,128]{2,1,0:T(8,128)S(1)} %convolution_bitcast_fusion.1, f32[36,16,64]{2,1,0:T(8,128)S(1)} %fusion.2, f32[36,64,128]{2,1,0:T(8,128)S(1)} %copy-done), kind=kOutput, calls=%fused_computation.5 | convolution fusion | flops 56696832 | bytes 1916928 | tf_op jit(solution)/shard_map/lrp,lvr->lvp/dot_general | solution.py:53
  (29 shorter events, 0.4 us)
Async XLA Ops:
  0.0 1.3 %copy-start = (f32[36,64,128]{2,1,0:T(8,128)S(1)}, f32[36,64,128]{2,1,0:T(8,128)}, u32[]{:S(2)}) copy-start(f32[36,64,128]{2,1,0:T(8,128)} %param.11) | copy-start | bytes 3538948
  0.0 19.1 %copy-start.7 = (s32[1,16]{1,0:T(1,128)S(1)}, s32[1,16]{1,0:T(1,128)}, u32[]{:S(2)}) copy-start(s32[1,16]{1,0:T(1,128)} %param.18) | copy-start | bytes 196
  0.0 19.1 %copy-start.5 = (s32[36,3]{0,1:T(4,128)S(1)}, s32[36,3]{0,1:T(4,128)}, u32[]{:S(2)}) copy-start(s32[36,3]{0,1:T(4,128)} %param.12) | copy-start | bytes 1300
  0.0 19.1 %copy-start.6 = (s32[36,4]{0,1:T(4,128)S(1)}, s32[36,4]{0,1:T(4,128)}, u32[]{:S(2)}) copy-start(s32[36,4]{0,1:T(4,128)} %param.14) | copy-start | bytes 1732
  0.0 19.6 %copy-start.1 = (f32[36,64,64]{2,1,0:T(8,128)S(1)}, f32[36,64,64]{2,1,0:T(8,128)}, u32[]{:S(2)}) copy-start(f32[36,64,64]{2,1,0:T(8,128)} %param.16) | copy-start | bytes 1769476
  4.2 16.5 %copy-start.2 = (f32[1,64,64]{2,1,0:T(8,128)S(1)}, f32[1,64,64]{2,1,0:T(8,128)}, u32[]{:S(2)}) copy-start(f32[1,64,64]{2,1,0:T(8,128)} %param.17) | copy-start | bytes 49156
  4.2 87.3 %collective-permute-start.3 = (f32[36,16,64]{2,1,0:T(8,128)S(1)}, f32[36,16,64]{2,1,0:T(8,128)}, u32[]{:S(2)}, u32[]{:S(2)}) collective-permute-start(f32[36,16,64]{2,1,0:T(8,128)S(1)} %fusion.21), channel_id=1, source_target_pairs={{1,0},{2,1},{3,2},{4,3},{5,4},{6,5},{7,6},{8,7},{9,8},{10,9},{11,1... | collective-permute-start | bytes 442376 | tf_op jit(solution)/shard_map/ppermute | solution.py:17
  10.3 81.2 %collective-permute-start.2 = (f32[36,16,64]{2,1,0:T(8,128)S(1)}, f32[36,16,64]{2,1,0:T(8,128)}, u32[]{:S(2)}, u32[]{:S(2)}) collective-permute-start(f32[36,16,64]{2,1,0:T(8,128)S(1)} %fusion.21), channel_id=1, source_target_pairs={{0,1},{1,2},{2,3},{3,4},{4,5},{5,6},{6,7},{7,8},{8,9},{9,10},{10,1... | collective-permute-start | bytes 442376 | tf_op jit(solution)/shard_map/ppermute | solution.py:14
  12.3 89.6 %collective-permute-start.1 = (f32[36,16,128]{2,1,0:T(8,128)}, f32[36,16,128]{2,1,0:T(8,128)}, u32[]{:S(2)}, u32[]{:S(2)}) collective-permute-start(f32[36,16,128]{2,1,0:T(8,128)} %param.10), channel_id=1, source_target_pairs={{1,0},{2,1},{3,2},{4,3},{5,4},{6,5},{7,6},{8,7},{9,8},{10,9},{11,1... | collective-permute-start | bytes 884744 | tf_op jit(solution)/shard_map/ppermute | solution.py:17
  17.1 84.7 %collective-permute-start = (f32[36,16,128]{2,1,0:T(8,128)}, f32[36,16,128]{2,1,0:T(8,128)}, u32[]{:S(2)}, u32[]{:S(2)}) collective-permute-start(f32[36,16,128]{2,1,0:T(8,128)} %param.10), channel_id=1, source_target_pairs={{0,1},{1,2},{2,3},{3,4},{4,5},{5,6},{6,7},{7,8},{8,9},{9,10},{10,1... | collective-permute-start | bytes 884744 | tf_op jit(solution)/shard_map/ppermute | solution.py:14
  92.6 1.8 %copy-start.4 = (pred[36,4]{1,0:T(8,128)(4,1)S(1)}, pred[36,4]{1,0:T(8,128)(4,1)}, u32[]{:S(2)}) copy-start(pred[36,4]{1,0:T(8,128)(4,1)} %copy.20) | copy-start | bytes 436
  103.1 0.7 copy-start.3
where the time goes:
time: 116 us; the launch traced here: 115 us
  blocking collectives  67 us (58%)
  matrix products  24.9 us (21%)
  starting transfers between devices  14.9 us (13%)
  local copies, waits for them, and re-layouts  6.18 us (5%)
  other arithmetic  2.37 us (2%)
    all_gather x1, blocking collectives, per_device(): nodes = lax.all_gather(branch_node[None], 'branch', axis=0, tiled=True)  56.7 us
    ppermute x2, starting transfers between devices, with_halo(): lax.ppermute(lax.slice_in_dim(block, 0, width, axis=dim), axis, backward)  11 us
    psum x1, blocking collectives, per_device(): branch_node = lax.psum(share, 'sub')  10.3 us
    dot_general x1, matrix products, per_device(): jnp.einsum('lkpq,lkvq->lvp', near_blocks, near_rows, precision=highest)  9.8 us
    dot_general x1, matrix products, per_device(): jnp.einsum('lkrs,lkvs->lvr', coupling_blocks, coupled_rows, precision=hig...  6.69 us
    ppermute x2, starting transfers between devices, with_halo(): lax.ppermute(lax.slice_in_dim(block, block.shape[dim] - width, None, axis...  3.85 us
    dot_general x1, matrix products, per_device(): coeffs = jnp.einsum('lrp,lvp->lvr', leaf_basis, vectors, precision=highest)  2.89 us
  transfers between devices with their start and end apart: 4, of which 0 were waited for; matrix products, arithmetic and copies ran while one was open for 14% of the time, Pallas kernels for 0%

commit v1 on v0

v1 whole, which is shorter than its diff:
```python
import jax
import jax.numpy as jnp
from jax import lax
from jax.experimental import pallas as pl
from jax.experimental.pallas import tpu as pltpu
from jax.sharding import PartitionSpec as P

MESH = pl.DeviceIdType.MESH
NT = (((1,), (1,)), ((), ()))
NN = (((1,), (0,)), ((), ()))
XS, ZS, CS, YS = 4, 8, 2, 4
L = 36
GROUP = 6


def split(x):
    hi = x.astype(jnp.bfloat16)
    lo = (x - hi.astype(jnp.float32)).astype(jnp.bfloat16)
    return hi, lo


def mm(a, b, dims):
    return lax.dot_general(a, b, dims, preferred_element_type=jnp.float32)


def dot3(a, b, dims):
    ah, al = split(a)
    bh, bl = split(b)
    rows = a.shape[0]
    both = mm(jnp.concatenate([ah, al], axis=0), bh, dims)
    return both[:rows] + (both[rows:] + mm(ah, bl, dims))


def pack(c):
    return jnp.concatenate([c[:8], c[8:]], axis=1)


def unpack(p):
    return jnp.concatenate([p[:, :64], p[:, 64:]], axis=0)


def groups(body, init=None):
    def step(g, carry):
        return body([g * GROUP + i for i in range(GROUP)], carry)

    return lax.fori_loop(0, L // GROUP, step, init)


def kernel(
    near_index,
    coup_index,
    branch_index,
    vec_hbm,
    basis_hbm,
    near_hbm,
    coup_hbm,
    lt_hbm,
    ct_hbm,
    bb_hbm,
    out,
    wide,
    cw,
    basis,
    near,
    coup,
    lt,
    ct,
    bb,
    shares,
    nodes,
    down,
    local_sem,
    halo_send,
    halo_recv,
    tree_send,
    tree_recv,
):
    b = lax.axis_index("branch")
    y = lax.axis_index("sub")
    core = lax.rem(b, CS)
    z = lax.rem(lax.div(b, CS), ZS)
    x = lax.div(b, CS * ZS)
    flat = b * YS + y
    total = XS * ZS * CS * YS
    right = lax.rem(flat + 1, total)
    left = lax.rem(flat + total - 1, total)
    right = (lax.div(right, YS), lax.rem(right, YS))
    left = (lax.div(left, YS), lax.rem(left, YS))
    y_peers = [(b, lax.rem(y + j, YS)) for j in range(1, YS)]
    z_peers = [((x * ZS + lax.rem(z + j, ZS)) * CS + core, y) for j in range(1, ZS)]
    x_peers = [((lax.rem(x + j, XS) * ZS + z) * CS + core, y) for j in range(1, XS)]
    core_peers = [(b + 1 - 2 * core, y)]

    def local(src, dst, n):
        return pltpu.make_async_copy(src, dst, local_sem.at[n])

    loads = [
        local(vec_hbm, wide.at[pl.ds(L, L)], 0),
        local(basis_hbm, basis, 1),
        local(lt_hbm, lt, 2),
        local(ct_hbm, ct, 3),
        local(bb_hbm, bb, 4),
        local(near_hbm, near, 5),
        local(coup_hbm, coup, 6),
    ]
    for load in loads:
        load.start()

    barrier = pltpu.get_barrier_semaphore()
    peers = [right, left] + y_peers + z_peers + x_peers + core_peers
    for peer in peers:
        pl.semaphore_signal(barrier, inc=1, device_id=peer, device_id_type=MESH)
    pl.semaphore_wait(barrier, len(peers))

    def remote(src, dst, send, recv, peer):
        return pltpu.make_async_remote_copy(
            src_ref=src, dst_ref=dst, send_sem=send, recv_sem=recv, device_id=peer, device_id_type=MESH
        )

    vec_halo = [
        remote(vec_hbm, wide.at[pl.ds(0, L)], halo_send.at[0], halo_recv.at[0], right),
        remote(vec_hbm, wide.at[pl.ds(2 * L, L)], halo_send.at[1], halo_recv.at[1], left),
    ]
    for copy in vec_halo:
        copy.start()

    loads[0].wait()
    loads[1].wait()
    loads[2].wait()
    loads[3].wait()

    def coeff_step(ls, acc):
        cs = [dot3(wide[L + l], basis[l], NT) for l in ls]
        for l, c in zip(ls, cs):
            cw[L + l] = pack(c)
        for l, c in zip(ls, cs):
            acc = acc + dot3(c, lt[l], NT)
        return acc

    cluster = groups(coeff_step, jnp.zeros((16, 64), jnp.float32))
    shares[y] = pack(dot3(cluster, ct[0], NT))

    y_copies = [
        remote(shares.at[y], shares.at[y], tree_send.at[n], tree_recv.at[n], peer)
        for n, peer in enumerate(y_peers)
    ]
    for copy in y_copies:
        copy.start()

    coeff_halo = [
        remote(cw.at[pl.ds(L, L)], cw.at[pl.ds(0, L)], halo_send.at[2], halo_recv.at[2], right),
        remote(cw.at[pl.ds(L, L)], cw.at[pl.ds(2 * L, L)], halo_send.at[3], halo_recv.at[3], left),
    ]
    for copy in coeff_halo:
        copy.start()

    loads[5].wait()

    def near_own(ls, carry):
        for l in ls:
            out[l] = dot3(wide[L + l], near[l, 0], NT)
        return carry

    groups(near_own)

    for copy in y_copies:
        copy.wait_recv()
    nodes[core, x, z] = (shares[0] + shares[1]) + (shares[2] + shares[3])
    z_copies = [
        remote(nodes.at[core, x, z], nodes.at[core, x, z], tree_send.at[3 + n], tree_recv.at[3 + n], peer)
        for n, peer in enumerate(z_peers)
    ]
    for copy in z_copies:
        copy.start()
    for copy in z_copies:
        copy.wait_recv()
    x_copies = [
        remote(nodes.at[core, x], nodes.at[core, x], tree_send.at[10 + n], tree_recv.at[10 + n], peer)
        for n, peer in enumerate(x_peers)
    ]
    for copy in x_copies:
        copy.start()
    for copy in x_copies:
        copy.wait_recv()
    core_copies = [
        remote(nodes.at[core], nodes.at[core], tree_send.at[13], tree_recv.at[13], core_peers[0])
    ]
    for copy in core_copies:
        copy.start()
    for copy in core_copies:
        copy.wait_recv()

    loads[4].wait()
    far = jnp.zeros((16, 64), jnp.float32)
    for k in range(16):
        i = branch_index[0, k]
        half = lax.div(i, CS)
        node = nodes[lax.rem(i, CS), lax.div(half, ZS), lax.rem(half, ZS)]
        far = far + dot3(unpack(node), bb[0, k], NT)
    cluster_down = dot3(far, ct[0], NN)

    def down_step(ls, carry):
        for l in ls:
            down[l] = dot3(cluster_down, lt[l], NN)
        return carry

    groups(down_step)

    for copy in vec_halo:
        copy.wait_recv()
    anchor = flat * L - L

    def place(index):
        return jnp.clip(index - anchor, 0, 3 * L - 1)

    def near_step(ls, carry):
        for l in ls:
            acc = out[l]
            for k in (1, 2):
                acc = acc + dot3(wide[place(near_index[k, l])], near[l, k], NT)
            out[l] = acc
        return carry

    groups(near_step)

    for copy in coeff_halo:
        copy.wait_recv()
    loads[6].wait()

    def far_step(ls, carry):
        totals = []
        for l in ls:
            acc = down[l]
            for k in range(4):
                acc = acc + dot3(unpack(cw[place(coup_index[k, l])]), coup[l, k], NT)
            totals.append(acc)
        for l, acc in zip(ls, totals):
            out[l] = out[l] + dot3(acc, basis[l], NN)
        return carry

    groups(far_step)

    for copy in vec_halo + coeff_halo + y_copies + z_copies + x_copies + core_copies:
        copy.wait_send()


def per_device(
    vectors,
    leaf_basis,
    near_index,
    near_blocks,
    coupling_index,
    coupling_blocks,
    leaf_transfer,
    cluster_transfer,
    branch_index,
    branch_blocks,
):
    smem = pl.BlockSpec(memory_space=pltpu.SMEM)
    anywhere = pl.BlockSpec(memory_space=pl.ANY)
    f32 = jnp.float32
    return pl.pallas_call(
        kernel,
        name="h2_product",
        out_shape=jax.ShapeDtypeStruct((L, 16, 128), f32),
        in_specs=[smem] * 3 + [anywhere] * 7,
        out_specs=pl.BlockSpec(memory_space=pltpu.VMEM),
        scratch_shapes=[
            pltpu.VMEM((3 * L, 16, 128), f32),
            pltpu.VMEM((3 * L, 8, 128), f32),
            pltpu.VMEM((L, 64, 128), f32),
            pltpu.VMEM((L, 3, 128, 128), f32),
            pltpu.VMEM((L, 4, 64, 64), f32),
            pltpu.VMEM((L, 64, 64), f32),
            pltpu.VMEM((1, 64, 64), f32),
            pltpu.VMEM((1, 16, 64, 64), f32),
            pltpu.VMEM((YS, 8, 128), f32),
            pltpu.VMEM((CS, XS, ZS, 8, 128), f32),
            pltpu.VMEM((L, 16, 64), f32),
            pltpu.SemaphoreType.DMA((7,)),
            pltpu.SemaphoreType.DMA((4,)),
            pltpu.SemaphoreType.DMA((4,)),
            pltpu.SemaphoreType.DMA((14,)),
            pltpu.SemaphoreType.DMA((14,)),
        ],
        compiler_params=pltpu.CompilerParams(
            collective_id=0, has_side_effects=True, vmem_limit_bytes=56 * 1024 * 1024
        ),
    )(
        near_index.T,
        coupling_index.T,
        branch_index,
        vectors,
        leaf_basis,
        near_blocks,
        coupling_blocks,
        leaf_transfer,
        cluster_transfer,
        branch_blocks,
    )


def solution(mesh):
    rows = ("branch", "sub")
    in_specs = (
        P(rows, None, None),
        P(rows, None, None),
        P(rows, None),
        P(rows, None, None, None),
        P(rows, None),
        P(rows, None, None, None),
        P(rows, None, None),
        P(rows, None, None),
        P("branch", None),
        P("branch", None, None, None),
    )
    return jax.shard_map(
        per_device, mesh=mesh, in_specs=in_specs, out_specs=P(rows, None, None), check_vma=False
    )
```

time: 116 us -> 44.2 us (0.38)
  blocking collectives: 67 us -> 0 us
  Pallas kernels: 0 us -> 42.4 us
  matrix products: 24.9 us -> 0 us
  starting transfers between devices: 14.9 us -> 0 us
  local copies, waits for them, and re-layouts: 6.18 us -> 1.69 us
  other arithmetic: 2.37 us -> 0 us
    all_gather x1 -> x0, blocking collectives: 56.7 us -> none  [per_device(): nodes = lax.all_gather(branch_node[None], 'branch', axis=0, tiled=True)]
    pallas_call x0 -> x1, Pallas kernels: none -> 42.4 us  [per_device(): pl.pallas_call(kernel, name='h2_product', out_shape=jax.ShapeDtypeStruct(...]
    dot_general x9 -> x0, matrix products: 24.9 us -> none  [the longest x1 9.8 us: per_device(): jnp.einsum('lkpq,lkvq->lvp', near_blocks, near_rows, precision=highest)]
    ppermute x4 -> x0, starting transfers between devices: 14.9 us -> none  [the longest x2 11 us: with_halo(): lax.ppermute(lax.slice_in_dim(block, 0, width, axis=dim), axis, backward)]
    psum x1 -> x0, blocking collectives: 10.3 us -> none  [per_device(): branch_node = lax.psum(share, 'sub')]
    gather x3 -> x0, local copies, waits for them, and re-layouts: 3.1 us -> none  [the longest x1 1.81 us: per_device(): coupled_rows = jnp.take(wide_coeffs, coupling_index - anchor, axis=0)]
    concatenate x2 -> x0, other arithmetic: 2.31 us -> none  [with_halo(): block = jnp.concatenate([low, block, high], axis=dim)]
    and x2 -> x0, local copies, waits for them, and re-layouts: 1.4 us -> none  [the longest x1 0.7 us: per_device(): near_rows = jnp.take(wide_points, near_index - anchor, axis=0)]
  transfers between devices with their start and end apart: 4 -> 0, of which waited for: 0 -> 0; matrix products, arithmetic and copies ran while one was open for 14% -> 0% of each run, Pallas kernels for 0% -> 0%
where the time goes in v1:
time: 44.2 us; the launch traced here: 44.1 us
  Pallas kernels  42.4 us (96%)
  local copies, waits for them, and re-layouts  1.69 us (4%)
    pallas_call x1, Pallas kernels, per_device(): pl.pallas_call(kernel, name='h2_product', out_shape=jax.ShapeDtypeStruct(...  42.4 us
    unnamed x1, local copies, waits for them, and re-layouts  1.69 us

profile of v1, /device:TPU:1, one launch (start us, length us, event | category | flops | bytes accessed | tf_op | source)
XLA Modules:
  0.0 44.1 jit_solution(1176920009214823047)
XLA Ops:
  0.0 42.4 %h2_product.1 = f32[36,16,128]{2,1,0:T(8,128)} custom-call(s32[3,36]{1,0:T(4,128)} %bitcast.2, s32[4,36]{1,0:T(4,128)} %bitcast.3, s32[1,16]{1,0:T(1,128)} %branch_index.1, f32[36,16,128]{2,1,0:T(8,128)} %vec_hbm.1, f32[36,64,128]{2,1,0:T(8,128)} %basis_hbm.1, f32[36,3,128,128]{3,2,1,0:T(8,128)} %near_hbm.1, f32[36,4,64,64]{3,2,1,0:T(8,128)} %coup_hbm.1, ...), custom_call_target="tpu_custom_call" | custom-call | tf_op jit(solution)/shard_map/h2_product/pallas_call | solution.py:262
  42.4 1.7 %copy.12 = f32[36,16,128]{2,1,0:T(8,128)} copy(f32[36,16,128]{2,1,0:T(8,128)} %h2_product.1) | data formatting | bytes 589824

commit v2 on v1

v2 whole, which is shorter than its diff:
```python
import jax
import jax.numpy as jnp
from jax import lax
from jax.experimental import pallas as pl
from jax.experimental.pallas import tpu as pltpu
from jax.sharding import PartitionSpec as P

MESH = pl.DeviceIdType.MESH
NT = (((1,), (1,)), ((), ()))
NN = (((1,), (0,)), ((), ()))
XS, ZS, CS, YS = 4, 8, 2, 4
L = 36
CHUNKS = 3
PART = L // CHUNKS
GROUP = 6
F32, BF16 = jnp.float32, jnp.bfloat16


def split(x):
    hi = x.astype(BF16)
    lo = (x - hi.astype(F32)).astype(BF16)
    return hi, lo


def stack(x):
    return jnp.concatenate(split(x), axis=0)


def mm(a, b, dims):
    return lax.dot_general(a, b, dims, preferred_element_type=F32)


def dot3(a, b, dims):
    return dot3_split(a, *split(b), dims)


def dot3_split(a, bh, bl, dims):
    ah, al = split(a)
    rows = a.shape[0]
    both = mm(jnp.concatenate([ah, al], axis=0), bh, dims)
    return both[:rows] + (both[rows:] + mm(ah, bl, dims))


def pack(c):
    return jnp.concatenate([c[:8], c[8:]], axis=1)


def unpack(p):
    return jnp.concatenate([p[:, :64], p[:, 64:]], axis=0)


def groups(body, size=GROUP):
    def step(g, carry):
        body([g * size + i for i in range(size)])
        return carry

    lax.fori_loop(0, L // size, step, 0)


def kernel(
    near_index,
    coup_index,
    branch_index,
    vec_hbm,
    basis_hbm,
    near_hbm,
    coup_hbm,
    lt_hbm,
    ct_hbm,
    bb_hbm,
    out,
    wide,
    cw,
    basis,
    near,
    coup,
    lt,
    ct,
    bb,
    nodes,
    fars,
    bbh,
    bbl,
    down,
    local_sem,
    halo_send,
    halo_recv,
    node_send,
    node_recv,
    far_send,
    far_recv,
    pair_send,
    pair_recv,
):
    b = lax.axis_index("branch")
    y = lax.axis_index("sub")
    core = lax.rem(b, CS)
    z = lax.rem(lax.div(b, CS), ZS)
    x = lax.div(b, CS * ZS)
    flat = b * YS + y
    total = XS * ZS * CS * YS
    right = lax.rem(flat + 1, total)
    left = lax.rem(flat + total - 1, total)
    right = (lax.div(right, YS), lax.rem(right, YS))
    left = (lax.div(left, YS), lax.rem(left, YS))
    mine = x * ZS + z
    slot = core * XS * ZS + mine
    sibling = (b + 1 - 2 * core, y)

    def plane_peer(j):
        px = lax.rem(x + lax.div(j, ZS), XS)
        pz = lax.rem(z + lax.rem(j, ZS), ZS)
        return ((px * ZS + pz) * CS + core, y)

    def row_peer(j):
        return (b, lax.rem(y + j, YS))

    def local(src, dst, n):
        return pltpu.make_async_copy(src, dst, local_sem.at[n])

    first = []
    for i in range(CHUNKS):
        part = pl.ds(i * PART, PART)
        first.append(
            [
                local(vec_hbm.at[part], wide.at[pl.ds(L + i * PART, PART)], 3 * i),
                local(basis_hbm.at[part], basis.at[part], 3 * i + 1),
                local(lt_hbm.at[part], lt.at[part], 3 * i + 2),
            ]
        )
    for loads in first:
        for load in loads:
            load.start()
    n = 3 * CHUNKS
    ct_load = local(ct_hbm, ct, n)
    bb_load = local(bb_hbm, bb, n + 1)
    near_load = local(near_hbm, near, n + 2)
    coup_load = local(coup_hbm, coup, n + 3)
    for load in (ct_load, bb_load, near_load, coup_load):
        load.start()

    barrier = pltpu.get_barrier_semaphore()

    def greet(peer):
        pl.semaphore_signal(barrier, inc=1, device_id=peer, device_id_type=MESH)

    greet(right)
    greet(left)
    greet(sibling)

    def greet_plane(j, carry):
        greet(plane_peer(j))
        return carry

    def greet_row(j, carry):
        greet(row_peer(j))
        return carry

    lax.fori_loop(1, XS * ZS, greet_plane, 0)
    lax.fori_loop(1, YS, greet_row, 0)

    acc = jnp.zeros((32, 128), F32)
    for i in range(CHUNKS):
        for load in first[i]:
            load.wait()
        ls = range(i * PART, (i + 1) * PART)
        cs = [dot3(wide[L + l], basis[l], NT) for l in ls]
        for l, c in zip(ls, cs):
            cw[L + l] = pack(c)
        for l, c in zip(ls, cs):
            acc = acc + mm(stack(c), stack(lt[l]), NT)
    cluster = (acc[:16, :64] + acc[16:, :64]) + (acc[:16, 64:] + acc[16:, 64:])
    ct_load.wait()
    nodes[slot] = pack(dot3(cluster, ct[0], NT))

    pl.semaphore_wait(barrier, 3 + (XS * ZS - 1) + (YS - 1))

    def remote(src, dst, send, recv, peer):
        return pltpu.make_async_remote_copy(
            src_ref=src, dst_ref=dst, send_sem=send, recv_sem=recv, device_id=peer, device_id_type=MESH
        )

    def node_copy(j):
        return remote(
            nodes.at[slot], nodes.at[slot], node_send.at[j], node_recv.at[j], plane_peer(j)
        )

    def far_copy(j):
        return remote(fars.at[y], fars.at[y], far_send.at[j], far_recv.at[j], row_peer(j))

    def pair_copy(j):
        rows = pl.ds((core * XS + lax.rem(x + j, XS)) * ZS, ZS)
        return remote(nodes.at[rows], nodes.at[rows], pair_send.at[j], pair_recv.at[j], sibling)

    def each(lo, hi, body):
        def step(j, carry):
            body(j)
            return carry

        lax.fori_loop(lo, hi, step, 0)

    each(1, XS * ZS, lambda j: node_copy(j).start())

    vec_halo = [
        remote(vec_hbm, wide.at[pl.ds(0, L)], halo_send.at[0], halo_recv.at[0], right),
        remote(vec_hbm, wide.at[pl.ds(2 * L, L)], halo_send.at[1], halo_recv.at[1], left),
    ]
    coeff_halo = [
        remote(cw.at[pl.ds(L, L)], cw.at[pl.ds(0, L)], halo_send.at[2], halo_recv.at[2], right),
        remote(cw.at[pl.ds(L, L)], cw.at[pl.ds(2 * L, L)], halo_send.at[3], halo_recv.at[3], left),
    ]
    for copy in vec_halo + coeff_halo:
        copy.start()

    bb_load.wait()
    for k in range(16):
        bbh[k], bbl[k] = split(bb[0, k])

    def down_step(ls):
        for l in ls:
            step = dot3(dot3(ct[0], lt[l], NN), basis[l], NN)
            hi, lo = split(step)
            down[l, 0:64] = hi
            down[l, 64:128] = hi
            down[l, 128:192] = lo

    groups(down_step)

    near_load.wait()

    def near_own(ls):
        for l in ls:
            out[l] = dot3(wide[L + l], near[l, 0], NT)

    groups(near_own)

    anchor = flat * L - L

    def place(index):
        return jnp.clip(index - anchor, 0, 3 * L - 1)

    for copy in vec_halo:
        copy.wait_recv()

    def near_step(ls):
        for l in ls:
            acc = out[l]
            for k in (1, 2):
                acc = acc + dot3(wide[place(near_index[k, l])], near[l, k], NT)
            out[l] = acc

    groups(near_step)

    for j in (0, 1, 3, 2):
        each(j * ZS + (j == 0), (j + 1) * ZS, lambda n: node_copy(n).wait_recv())
        pair_copy((XS - j) % XS).start()
    each(0, XS, lambda j: pair_copy(j).wait_recv())

    far = jnp.zeros((16, 64), F32)
    for k in range(16):
        i = branch_index[0, k]
        node = nodes[lax.rem(i, CS) * (XS * ZS) + lax.div(i, CS)]
        far = far + dot3_split(unpack(node), bbh[k], bbl[k], NT)
    fars[y] = pack(far)
    each(1, YS, lambda j: far_copy(j).start())

    for copy in coeff_halo:
        copy.wait_recv()
    coup_load.wait()

    def far_step(ls):
        totals = []
        for l in ls:
            acc = jnp.zeros((16, 64), F32)
            for k in range(4):
                acc = acc + dot3(unpack(cw[place(coup_index[k, l])]), coup[l, k], NT)
            totals.append(acc)
        for l, acc in zip(ls, totals):
            out[l] = out[l] + dot3(acc, basis[l], NN)

    groups(far_step)

    each(1, YS, lambda j: far_copy(j).wait_recv())
    far = unpack((fars[0] + fars[1]) + (fars[2] + fars[3]))
    fh, fl = split(far)
    flh = jnp.concatenate([fh, fl, fh], axis=1)
    for l in range(L):
        out[l] = out[l] + mm(flh, down[l], NN)

    for copy in vec_halo + coeff_halo:
        copy.wait_send()
    each(1, XS * ZS, lambda j: node_copy(j).wait_send())
    each(1, YS, lambda j: far_copy(j).wait_send())
    each(0, XS, lambda j: pair_copy(j).wait_send())


def per_device(
    vectors,
    leaf_basis,
    near_index,
    near_blocks,
    coupling_index,
    coupling_blocks,
    leaf_transfer,
    cluster_transfer,
    branch_index,
    branch_blocks,
):
    smem = pl.BlockSpec(memory_space=pltpu.SMEM)
    anywhere = pl.BlockSpec(memory_space=pl.ANY)
    return pl.pallas_call(
        kernel,
        name="h2_product",
        out_shape=jax.ShapeDtypeStruct((L, 16, 128), F32),
        in_specs=[smem] * 3 + [anywhere] * 7,
        out_specs=pl.BlockSpec(memory_space=pltpu.VMEM),
        scratch_shapes=[
            pltpu.VMEM((3 * L, 16, 128), F32),
            pltpu.VMEM((3 * L, 8, 128), F32),
            pltpu.VMEM((L, 64, 128), F32),
            pltpu.VMEM((L, 3, 128, 128), F32),
            pltpu.VMEM((L, 4, 64, 64), F32),
            pltpu.VMEM((L, 64, 64), F32),
            pltpu.VMEM((1, 64, 64), F32),
            pltpu.VMEM((1, 16, 64, 64), F32),
            pltpu.VMEM((CS * XS * ZS, 8, 128), F32),
            pltpu.VMEM((YS, 8, 128), F32),
            pltpu.VMEM((16, 64, 64), BF16),
            pltpu.VMEM((16, 64, 64), BF16),
            pltpu.VMEM((L, 192, 128), BF16),
            pltpu.SemaphoreType.DMA((3 * CHUNKS + 4,)),
            pltpu.SemaphoreType.DMA((4,)),
            pltpu.SemaphoreType.DMA((4,)),
            pltpu.SemaphoreType.DMA((XS * ZS,)),
            pltpu.SemaphoreType.DMA((XS * ZS,)),
            pltpu.SemaphoreType.DMA((YS,)),
            pltpu.SemaphoreType.DMA((YS,)),
            pltpu.SemaphoreType.DMA((XS,)),
            pltpu.SemaphoreType.DMA((XS,)),
        ],
        compiler_params=pltpu.CompilerParams(
            collective_id=0, has_side_effects=True, vmem_limit_bytes=56 * 1024 * 1024
        ),
    )(
        near_index.T,
        coupling_index.T,
        branch_index,
        vectors,
        leaf_basis,
        near_blocks,
        coupling_blocks,
        leaf_transfer,
        cluster_transfer,
        branch_blocks,
    )


def solution(mesh):
    rows = ("branch", "sub")
    in_specs = (
        P(rows, None, None),
        P(rows, None, None),
        P(rows, None),
        P(rows, None, None, None),
        P(rows, None),
        P(rows, None, None, None),
        P(rows, None, None),
        P(rows, None, None),
        P("branch", None),
        P("branch", None, None, None),
    )
    return jax.shard_map(
        per_device, mesh=mesh, in_specs=in_specs, out_specs=P(rows, None, None), check_vma=False
    )
```

time: 44.2 us -> 37.2 us (0.84)
  Pallas kernels: 42.4 us -> 35.3 us
    pallas_call x1, Pallas kernels: 42.4 us -> 35.3 us  [per_device(): pl.pallas_call(kernel, name='h2_product', out_shape=jax.ShapeDtypeStruct(...]
where the time goes in v2:
time: 37.2 us; the launch traced here: 37 us
  Pallas kernels  35.3 us (95%)
  local copies, waits for them, and re-layouts  1.69 us (5%)
    pallas_call x1, Pallas kernels, per_device(): pl.pallas_call(kernel, name='h2_product', out_shape=jax.ShapeDtypeStruct(...  35.3 us
    unnamed x1, local copies, waits for them, and re-layouts  1.69 us

profile of v2, /device:TPU:1, one launch (start us, length us, event | category | flops | bytes accessed | tf_op | source)
XLA Modules:
  0.0 37.0 jit_solution(7287488882442148304)
XLA Ops:
  0.0 35.3 %h2_product.1 = f32[36,16,128]{2,1,0:T(8,128)} custom-call(s32[3,36]{1,0:T(4,128)} %bitcast.2, s32[4,36]{1,0:T(4,128)} %bitcast.3, s32[1,16]{1,0:T(1,128)} %branch_index.1, f32[36,16,128]{2,1,0:T(8,128)} %vec_hbm.1, f32[36,64,128]{2,1,0:T(8,128)} %basis_hbm.1, f32[36,3,128,128]{3,2,1,0:T(8,128)} %near_hbm.1, f32[36,4,64,64]{3,2,1,0:T(8,128)} %coup_hbm.1, ...), custom_call_target="tpu_custom_call" | custom-call | tf_op jit(solution)/shard_map/h2_product/pallas_call | solution.py:311
  35.3 1.7 %copy.12 = f32[36,16,128]{2,1,0:T(8,128)} copy(f32[36,16,128]{2,1,0:T(8,128)} %h2_product.1) | data formatting | bytes 589824

commit v3 on v2

--- a/solution.py
+++ b/solution.py
@@ -12,7 +12,7 @@
 L = 36
 CHUNKS = 3
 PART = L // CHUNKS
-GROUP = 6
+GROUP = 12
 F32, BF16 = jnp.float32, jnp.bfloat16
 
 
@@ -47,6 +47,24 @@
 
 def unpack(p):
     return jnp.concatenate([p[:, :64], p[:, 64:]], axis=0)
+
+
+def pair(p, q):
+    low = lax.broadcasted_iota(jnp.int32, p.shape, 1) < 64
+    top = jnp.where(low, p, pltpu.roll(q, 64, 1))
+    bottom = jnp.where(low, pltpu.roll(p, 64, 1), q)
+    return jnp.concatenate([top, bottom], axis=0)
+
+
+def fold(s):
+    half = s.shape[1] // 2
+    both = s[:16] + s[16:]
+    return both[:, :half] + both[:, half:]
+
+
+def wide_split(x):
+    hi = x.astype(BF16).astype(F32)
+    return jnp.concatenate([hi, x - hi], axis=1).astype(BF16)
 
 
 def groups(body, size=GROUP):
@@ -82,6 +100,9 @@
     bbh,
     bbl,
     down,
+    near12,
+    coup4,
+    basis2,
     local_sem,
     halo_send,
     halo_recv,
@@ -199,8 +220,6 @@
 
         lax.fori_loop(lo, hi, step, 0)
 
-    each(1, XS * ZS, lambda j: node_copy(j).start())
-
     vec_halo = [
         remote(vec_hbm, wide.at[pl.ds(0, L)], halo_send.at[0], halo_recv.at[0], right),
         remote(vec_hbm, wide.at[pl.ds(2 * L, L)], halo_send.at[1], halo_recv.at[1], left),
@@ -209,8 +228,15 @@
         remote(cw.at[pl.ds(L, L)], cw.at[pl.ds(0, L)], halo_send.at[2], halo_recv.at[2], right),
         remote(cw.at[pl.ds(L, L)], cw.at[pl.ds(2 * L, L)], halo_send.at[3], halo_recv.at[3], left),
     ]
-    for copy in vec_halo + coeff_halo:
-        copy.start()
+    early = z < ZS // 2
+
+    def start_halos():
+        for copy in vec_halo + coeff_halo:
+            copy.start()
+
+    pl.when(early)(start_halos)
+    each(1, XS * ZS, lambda j: node_copy(j).start())
+    pl.when(jnp.logical_not(early))(start_halos)
 
     bb_load.wait()
     for k in range(16):
@@ -231,8 +257,21 @@
     def near_own(ls):
         for l in ls:
             out[l] = dot3(wide[L + l], near[l, 0], NT)
+        for l in ls:
+            for k in (1, 2):
+                near12[l, (k - 1) * 128 : k * 128] = wide_split(near[l, k].T)
 
     groups(near_own)
+
+    coup_load.wait()
+
+    def coup_own(ls):
+        for l in ls:
+            for k in range(4):
+                coup4[l, k * 64 : (k + 1) * 64] = wide_split(coup[l, k].T)
+            basis2[l] = wide_split(basis[l])
+
+    groups(coup_own)
 
     anchor = flat * L - L
 
@@ -244,10 +283,12 @@
 
     def near_step(ls):
         for l in ls:
-            acc = out[l]
-            for k in (1, 2):
-                acc = acc + dot3(wide[place(near_index[k, l])], near[l, k], NT)
-            out[l] = acc
+            h1, l1 = split(wide[place(near_index[1, l])])
+            h2, l2 = split(wide[place(near_index[2, l])])
+            rows = jnp.concatenate(
+                [jnp.concatenate([h1, h2], axis=1), jnp.concatenate([l1, l2], axis=1)], axis=0
+            )
+            out[l] = out[l] + fold(mm(rows, near12[l], NN))
 
     groups(near_step)
 
@@ -266,17 +307,15 @@
 
     for copy in coeff_halo:
         copy.wait_recv()
-    coup_load.wait()
 
     def far_step(ls):
         totals = []
         for l in ls:
-            acc = jnp.zeros((16, 64), F32)
-            for k in range(4):
-                acc = acc + dot3(unpack(cw[place(coup_index[k, l])]), coup[l, k], NT)
-            totals.append(acc)
+            p = [cw[place(coup_index[k, l])] for k in range(4)]
+            rows = stack(jnp.concatenate([pair(p[0], p[1]), pair(p[2], p[3])], axis=1))
+            totals.append(fold(mm(rows, coup4[l], NN)))
         for l, acc in zip(ls, totals):
-            out[l] = out[l] + dot3(acc, basis[l], NN)
+            out[l] = out[l] + fold(mm(stack(acc), basis2[l], NN))
 
     groups(far_step)
 
@@ -328,6 +367,9 @@
             pltpu.VMEM((16, 64, 64), BF16),
             pltpu.VMEM((16, 64, 64), BF16),
             pltpu.VMEM((L, 192, 128), BF16),
+            pltpu.VMEM((L, 256, 256), BF16),
+            pltpu.VMEM((L, 256, 128), BF16),
+            pltpu.VMEM((L, 64, 256), BF16),
             pltpu.SemaphoreType.DMA((3 * CHUNKS + 4,)),
             pltpu.SemaphoreType.DMA((4,)),
             pltpu.SemaphoreType.DMA((4,)),

time: 37.2 us -> 32.7 us (0.88)
  Pallas kernels: 35.3 us -> 30.8 us
    pallas_call x1, Pallas kernels: 35.3 us -> 30.8 us  [per_device(): pl.pallas_call(kernel, name='h2_product', out_shape=jax.ShapeDtypeStruct(...]
where the time goes in v3:
time: 32.7 us; the launch traced here: 32.5 us
  Pallas kernels  30.8 us (94%)
  local copies, waits for them, and re-layouts  1.69 us (5%)
    pallas_call x1, Pallas kernels, per_device(): pl.pallas_call(kernel, name='h2_product', out_shape=jax.ShapeDtypeStruct(...  30.8 us
    unnamed x1, local copies, waits for them, and re-layouts  1.69 us

profile of v3, /device:TPU:1, one launch (start us, length us, event | category | flops | bytes accessed | tf_op | source)
XLA Modules:
  0.0 32.5 jit_solution(10095383098448883222)
XLA Ops:
  0.0 30.8 %h2_product.1 = f32[36,16,128]{2,1,0:T(8,128)} custom-call(s32[3,36]{1,0:T(4,128)} %bitcast.2, s32[4,36]{1,0:T(4,128)} %bitcast.3, s32[1,16]{1,0:T(1,128)} %branch_index.1, f32[36,16,128]{2,1,0:T(8,128)} %vec_hbm.1, f32[36,64,128]{2,1,0:T(8,128)} %basis_hbm.1, f32[36,3,128,128]{3,2,1,0:T(8,128)} %near_hbm.1, f32[36,4,64,64]{3,2,1,0:T(8,128)} %coup_hbm.1, ...), custom_call_target="tpu_custom_call" | custom-call | tf_op jit(solution)/shard_map/h2_product/pallas_call | solution.py:350
  30.8 1.7 %copy.12 = f32[36,16,128]{2,1,0:T(8,128)} copy(f32[36,16,128]{2,1,0:T(8,128)} %h2_product.1) | data formatting | bytes 589824

commit v4 on v3

--- a/solution.py
+++ b/solution.py
@@ -290,7 +290,7 @@
             )
             out[l] = out[l] + fold(mm(rows, near12[l], NN))
 
-    groups(near_step)
+    groups(near_step, 18)
 
     for j in (0, 1, 3, 2):
         each(j * ZS + (j == 0), (j + 1) * ZS, lambda n: node_copy(n).wait_recv())
@@ -317,7 +317,7 @@
         for l, acc in zip(ls, totals):
             out[l] = out[l] + fold(mm(stack(acc), basis2[l], NN))
 
-    groups(far_step)
+    groups(far_step, 18)
 
     each(1, YS, lambda j: far_copy(j).wait_recv())
     far = unpack((fars[0] + fars[1]) + (fars[2] + fars[3]))
@@ -331,6 +331,12 @@
     each(1, XS * ZS, lambda j: node_copy(j).wait_send())
     each(1, YS, lambda j: far_copy(j).wait_send())
     each(0, XS, lambda j: pair_copy(j).wait_send())
+
+
+def store(source, target, sem):
+    copy = pltpu.make_async_copy(source, target, sem)
+    copy.start()
+    copy.wait()
 
 
 def per_device(
@@ -347,10 +353,10 @@
 ):
     smem = pl.BlockSpec(memory_space=pltpu.SMEM)
     anywhere = pl.BlockSpec(memory_space=pl.ANY)
-    return pl.pallas_call(
+    result = pl.pallas_call(
         kernel,
         name="h2_product",
-        out_shape=jax.ShapeDtypeStruct((L, 16, 128), F32),
+        out_shape=pltpu.VMEM((L, 16, 128), F32),
         in_specs=[smem] * 3 + [anywhere] * 7,
         out_specs=pl.BlockSpec(memory_space=pltpu.VMEM),
         scratch_shapes=[
@@ -395,6 +401,15 @@
         cluster_transfer,
         branch_blocks,
     )
+    result = pltpu.with_memory_space_constraint(result, pltpu.VMEM)
+    return pl.pallas_call(
+        store,
+        name="store",
+        out_shape=jax.ShapeDtypeStruct((L, 16, 128), F32),
+        in_specs=[pl.BlockSpec(memory_space=pltpu.VMEM)],
+        out_specs=anywhere,
+        scratch_shapes=[pltpu.SemaphoreType.DMA],
+    )(result)
 
 
 def solution(mesh):

time: 32.7 us -> 30.8 us (0.942)
  local copies, waits for them, and re-layouts: 1.69 us -> 0 us
    unnamed x1 -> x0, local copies, waits for them, and re-layouts: 1.69 us -> none
    pallas_call x1 -> x2, Pallas kernels: 30.8 us -> 30.7 us  [the longest x1 30 us: per_device(): pl.pallas_call(kernel, name='h2_product', out_shape=pltpu.VMEM((L, 16, 12...]
where the time goes in v4:
time: 30.8 us; the launch traced here: 30.7 us
  Pallas kernels  30.7 us (100%)
    pallas_call x1, Pallas kernels, per_device(): pl.pallas_call(kernel, name='h2_product', out_shape=pltpu.VMEM((L, 16, 12...  30 us
    pallas_call x1, Pallas kernels, per_device(): pl.pallas_call(store, name='store', out_shape=jax.ShapeDtypeStruct((L, 16...  0.72 us

profile of v4, /device:TPU:1, one launch (start us, length us, event | category | flops | bytes accessed | tf_op | source)
XLA Modules:
  0.0 30.7 jit_solution(4910883253529801721)
XLA Ops:
  0.0 30.0 %h2_product.1.source = f32[36,16,128]{2,1,0:T(8,128)S(1)} custom-call(s32[3,36]{1,0:T(4,128)} %bitcast.2, s32[4,36]{1,0:T(4,128)} %bitcast.3, s32[1,16]{1,0:T(1,128)} %branch_index.1, f32[36,16,128]{2,1,0:T(8,128)} %vec_hbm.1, f32[36,64,128]{2,1,0:T(8,128)} %basis_hbm.1, f32[36,3,128,128]{3,2,1,0:T(8,128)} %near_hbm.1, f32[36,4,64,64]{3,2,1,0:T(8,128)} %coup_hbm.1, ...), custom_call_target="tpu_custom_call" | custom-call | tf_op jit(solution)/shard_map/h2_product/pallas_call | solution.py:356
  30.0 0.7 %store.1 = f32[36,16,128]{2,1,0:T(8,128)} custom-call(f32[36,16,128]{2,1,0:T(8,128)S(1)} %h2_product.1.source), custom_call_target="tpu_custom_call" | custom-call | tf_op jit(solution)/shard_map/store/pallas_call | solution.py:405

commit v5 on v4

--- a/solution.py
+++ b/solution.py
@@ -133,11 +133,37 @@
         pz = lax.rem(z + lax.rem(j, ZS), ZS)
         return ((px * ZS + pz) * CS + core, y)
 
+    def far_first(n):
+        q = lax.div(n, XS)
+        sign = 1 - 2 * lax.rem(q, 2)
+        dz = lax.rem(ZS // 2 + sign * lax.div(q + 1, 2) + ZS, ZS)
+        return (XS - 1 - lax.rem(n, XS)) * ZS + dz
+
     def row_peer(j):
         return (b, lax.rem(y + j, YS))
 
     def local(src, dst, n):
         return pltpu.make_async_copy(src, dst, local_sem.at[n])
+
+    barrier = pltpu.get_barrier_semaphore()
+
+    def greet(peer):
+        pl.semaphore_signal(barrier, inc=1, device_id=peer, device_id_type=MESH)
+
+
+    def greet_plane(n, carry):
+        greet(plane_peer(far_first(n)))
+        return carry
+
+    def greet_row(j, carry):
+        greet(row_peer(j))
+        return carry
+
+    lax.fori_loop(0, XS * ZS - 1, greet_plane, 0)
+    greet(right)
+    greet(left)
+    greet(sibling)
+    lax.fori_loop(1, YS, greet_row, 0)
 
     first = []
     for i in range(CHUNKS):
@@ -160,26 +186,6 @@
     for load in (ct_load, bb_load, near_load, coup_load):
         load.start()
 
-    barrier = pltpu.get_barrier_semaphore()
-
-    def greet(peer):
-        pl.semaphore_signal(barrier, inc=1, device_id=peer, device_id_type=MESH)
-
-    greet(right)
-    greet(left)
-    greet(sibling)
-
-    def greet_plane(j, carry):
-        greet(plane_peer(j))
-        return carry
-
-    def greet_row(j, carry):
-        greet(row_peer(j))
-        return carry
-
-    lax.fori_loop(1, XS * ZS, greet_plane, 0)
-    lax.fori_loop(1, YS, greet_row, 0)
-
     acc = jnp.zeros((32, 128), F32)
     for i in range(CHUNKS):
         for load in first[i]:
@@ -231,11 +237,11 @@
     early = z < ZS // 2
 
     def start_halos():
-        for copy in vec_halo + coeff_halo:
+        for copy in coeff_halo + vec_halo:
             copy.start()
 
     pl.when(early)(start_halos)
-    each(1, XS * ZS, lambda j: node_copy(j).start())
+    each(0, XS * ZS - 1, lambda n: node_copy(far_first(n)).start())
     pl.when(jnp.logical_not(early))(start_halos)
 
     bb_load.wait()
@@ -278,19 +284,19 @@
     def place(index):
         return jnp.clip(index - anchor, 0, 3 * L - 1)
 
-    for copy in vec_halo:
+    for copy in coeff_halo:
         copy.wait_recv()
 
-    def near_step(ls):
-        for l in ls:
-            h1, l1 = split(wide[place(near_index[1, l])])
-            h2, l2 = split(wide[place(near_index[2, l])])
-            rows = jnp.concatenate(
-                [jnp.concatenate([h1, h2], axis=1), jnp.concatenate([l1, l2], axis=1)], axis=0
-            )
-            out[l] = out[l] + fold(mm(rows, near12[l], NN))
-
-    groups(near_step, 18)
+    def far_step(ls):
+        totals = []
+        for l in ls:
+            p = [cw[place(coup_index[k, l])] for k in range(4)]
+            rows = stack(jnp.concatenate([pair(p[0], p[1]), pair(p[2], p[3])], axis=1))
+            totals.append(fold(mm(rows, coup4[l], NN)))
+        for l, acc in zip(ls, totals):
+            out[l] = out[l] + fold(mm(stack(acc), basis2[l], NN))
+
+    groups(far_step, 18)
 
     for j in (0, 1, 3, 2):
         each(j * ZS + (j == 0), (j + 1) * ZS, lambda n: node_copy(n).wait_recv())
@@ -305,19 +311,19 @@
     fars[y] = pack(far)
     each(1, YS, lambda j: far_copy(j).start())
 
-    for copy in coeff_halo:
+    for copy in vec_halo:
         copy.wait_recv()
 
-    def far_step(ls):
-        totals = []
-        for l in ls:
-            p = [cw[place(coup_index[k, l])] for k in range(4)]
-            rows = stack(jnp.concatenate([pair(p[0], p[1]), pair(p[2], p[3])], axis=1))
-            totals.append(fold(mm(rows, coup4[l], NN)))
-        for l, acc in zip(ls, totals):
-            out[l] = out[l] + fold(mm(stack(acc), basis2[l], NN))
-
-    groups(far_step, 18)
+    def near_step(ls):
+        for l in ls:
+            h1, l1 = split(wide[place(near_index[1, l])])
+            h2, l2 = split(wide[place(near_index[2, l])])
+            rows = jnp.concatenate(
+                [jnp.concatenate([h1, h2], axis=1), jnp.concatenate([l1, l2], axis=1)], axis=0
+            )
+            out[l] = out[l] + fold(mm(rows, near12[l], NN))
+
+    groups(near_step, 18)
 
     each(1, YS, lambda j: far_copy(j).wait_recv())
     far = unpack((fars[0] + fars[1]) + (fars[2] + fars[3]))

time: 30.8 us -> 29.2 us (0.948)
  Pallas kernels: 30.7 us -> 29.1 us
    pallas_call x1, Pallas kernels: 30 us -> 28.3 us  [per_device(): pl.pallas_call(kernel, name='h2_product', out_shape=pltpu.VMEM((L, 16, 12...]
where the time goes in v5:
time: 29.2 us; the launch traced here: 29.1 us
  Pallas kernels  29.1 us (100%)
    pallas_call x1, Pallas kernels, per_device(): pl.pallas_call(kernel, name='h2_product', out_shape=pltpu.VMEM((L, 16, 12...  28.3 us
    pallas_call x1, Pallas kernels, per_device(): pl.pallas_call(store, name='store', out_shape=jax.ShapeDtypeStruct((L, 16...  0.72 us

profile of v5, /device:TPU:1, one launch (start us, length us, event | category | flops | bytes accessed | tf_op | source)
XLA Modules:
  0.0 29.1 jit_solution(7708664892467655421)
XLA Ops:
  0.0 28.3 %h2_product.1.source = f32[36,16,128]{2,1,0:T(8,128)S(1)} custom-call(s32[3,36]{1,0:T(4,128)} %bitcast.2, s32[4,36]{1,0:T(4,128)} %bitcast.3, s32[1,16]{1,0:T(1,128)} %branch_index.1, f32[36,16,128]{2,1,0:T(8,128)} %vec_hbm.1, f32[36,64,128]{2,1,0:T(8,128)} %basis_hbm.1, f32[36,3,128,128]{3,2,1,0:T(8,128)} %near_hbm.1, f32[36,4,64,64]{3,2,1,0:T(8,128)} %coup_hbm.1, ...), custom_call_target="tpu_custom_call" | custom-call | tf_op jit(solution)/shard_map/h2_product/pallas_call | solution.py:362
  28.3 0.7 %store.1 = f32[36,16,128]{2,1,0:T(8,128)} custom-call(f32[36,16,128]{2,1,0:T(8,128)S(1)} %h2_product.1.source), custom_call_target="tpu_custom_call" | custom-call | tf_op jit(solution)/shard_map/store/pallas_call | solution.py:411

commit v6 on v5

--- a/solution.py
+++ b/solution.py
@@ -296,7 +296,7 @@
         for l, acc in zip(ls, totals):
             out[l] = out[l] + fold(mm(stack(acc), basis2[l], NN))
 
-    groups(far_step, 18)
+    groups(far_step, 36)
 
     for j in (0, 1, 3, 2):
         each(j * ZS + (j == 0), (j + 1) * ZS, lambda n: node_copy(n).wait_recv())
@@ -311,6 +311,10 @@
     fars[y] = pack(far)
     each(1, YS, lambda j: far_copy(j).start())
 
+    each(1, XS * ZS, lambda j: node_copy(j).wait_send())
+    each(0, XS, lambda j: pair_copy(j).wait_send())
+    for copy in coeff_halo:
+        copy.wait_send()
     for copy in vec_halo:
         copy.wait_recv()
 
@@ -323,7 +327,7 @@
             )
             out[l] = out[l] + fold(mm(rows, near12[l], NN))
 
-    groups(near_step, 18)
+    groups(near_step, 36)
 
     each(1, YS, lambda j: far_copy(j).wait_recv())
     far = unpack((fars[0] + fars[1]) + (fars[2] + fars[3]))
@@ -332,11 +336,9 @@
     for l in range(L):
         out[l] = out[l] + mm(flh, down[l], NN)
 
-    for copy in vec_halo + coeff_halo:
+    for copy in vec_halo:
         copy.wait_send()
-    each(1, XS * ZS, lambda j: node_copy(j).wait_send())
     each(1, YS, lambda j: far_copy(j).wait_send())
-    each(0, XS, lambda j: pair_copy(j).wait_send())
 
 
 def store(source, target, sem):

time: 29.2 us -> 28.8 us (0.986)
  Pallas kernels: 29.1 us -> 28.7 us
    pallas_call x1, Pallas kernels: 28.3 us -> 28 us  [per_device(): pl.pallas_call(kernel, name='h2_product', out_shape=pltpu.VMEM((L, 16, 12...]
where the time goes in v6:
time: 28.8 us; the launch traced here: 28.7 us
  Pallas kernels  28.7 us (100%)
    pallas_call x1, Pallas kernels, per_device(): pl.pallas_call(kernel, name='h2_product', out_shape=pltpu.VMEM((L, 16, 12...  28 us
    pallas_call x1, Pallas kernels, per_device(): pl.pallas_call(store, name='store', out_shape=jax.ShapeDtypeStruct((L, 16...  0.72 us

profile of v6, /device:TPU:1, one launch (start us, length us, event | category | flops | bytes accessed | tf_op | source)
XLA Modules:
  0.0 28.7 jit_solution(11726553712060784605)
XLA Ops:
  0.0 28.0 %h2_product.1.source = f32[36,16,128]{2,1,0:T(8,128)S(1)} custom-call(s32[3,36]{1,0:T(4,128)} %bitcast.2, s32[4,36]{1,0:T(4,128)} %bitcast.3, s32[1,16]{1,0:T(1,128)} %branch_index.1, f32[36,16,128]{2,1,0:T(8,128)} %vec_hbm.1, f32[36,64,128]{2,1,0:T(8,128)} %basis_hbm.1, f32[36,3,128,128]{3,2,1,0:T(8,128)} %near_hbm.1, f32[36,4,64,64]{3,2,1,0:T(8,128)} %coup_hbm.1, ...), custom_call_target="tpu_custom_call" | custom-call | tf_op jit(solution)/shard_map/h2_product/pallas_call | solution.py:364
  28.0 0.7 %store.1 = f32[36,16,128]{2,1,0:T(8,128)} custom-call(f32[36,16,128]{2,1,0:T(8,128)S(1)} %h2_product.1.source), custom_call_target="tpu_custom_call" | custom-call | tf_op jit(solution)/shard_map/store/pallas_call | solution.py:413
